TPU v7x, 32 devices: a whole 2x2x4 slice. The times are simulated.
32 devices in a mesh: member: 4 (over y, x), shard: 8 (over z, core).
Axes of the slice: x: 2, y: 2, z: 4, core: 2. Of those that a mesh axis runs over, the one named last changes fastest.
Arguments:
- trunk_out: bfloat16 [128, 8192], P('shard', 'member'), may hold values from -6 to 6
- segment_ids: int32 [128], replicated, may hold values from 0 to 7, never falling along the last dimension, each value on 1 to 32 neighbouring positions
- pair_order: int32 [8], replicated, may hold values from 0 to 7, each once
- w_query: bfloat16 [4, 8, 4096, 128], P('member', 'shard'), may hold values from -0.25 to 0.25
- w_key_value: bfloat16 [4, 8, 1024, 256], P('member', 'shard'), may hold values from -0.0625 to 0.0625
- w_out: bfloat16 [4, 512, 8192], P('member', 'shard'), may hold values from -0.25 to 0.25
- norm_gain: float32 [4, 8192], P('member'), may hold values from 0.1 to 1.9
- reward_weight: float32 [4, 8192], P('member'), may hold values from -0.0625 to 0.0625
Outputs:
- trunk_grad: float32 [128, 8192], P('member', 'shard')
- rewards: float32 [4, 8], P('member')
Inputs may be any that keep to these rules, and one draw needn't show every extreme that they name: `segment_ids`: segment numbers never fall along the tokens; every sequence 0 to 7 has 1 to 32 tokens, and one has exactly 32. Each sequence appears once; sequence pair_order[2 * i] is preferred to sequence pair_order[2 * i + 1].
All inputs are finite; a program needn't handle non-finite values.
Results may differ from a plain program's by a relative error of at most 0.011.
Values may be sent and summed in bfloat16 or wider, within the bound.
No kernel may reach another device: no remote copies, remote signals or barrier semaphores. Data moves between devices by JAX's collectives and lax.ppermute only.
A program may use at most 64 MiB of HBM per device.

v0:
```python
import math
import jax
import jax.numpy as jnp
from jax import lax
from jax.sharding import PartitionSpec as P

HD = 128
SEQS = 8
softcap_limit = 20.0
loss_scale = 256.0
norm_eps = 1e-05


def from_partner(block, axis, stride):
    count = lax.axis_size(axis)
    route = []
    for low in range(count):
        high = low | 1 << stride
        if high != low and high < count:
            route += [(low, high), (high, low)]
    return lax.ppermute(block, axis, route)


def partner_swap(values, bit_number):
    return from_partner(values, "shard", bit_number)


def group_total(values, bit_list):
    for bit_number in bit_list:
        values = values + partner_swap(values, bit_number)
    return values


def pair_join(own_part, other_part, pair_side, join_axis):
    first_part = jnp.where(pair_side == 0, own_part, other_part)
    second_part = jnp.where(pair_side == 0, other_part, own_part)
    return jnp.concatenate([first_part, second_part], axis=join_axis)


def on_device(
    trunk_out, segment_ids, pair_order, w_query, w_key_value, w_out, norm_gain, reward_weight
):
    n_shard = lax.axis_size("shard")
    query_heads = n_shard // 2
    kv_count = max(1, query_heads // 8)
    group_size = query_heads // kv_count
    shard_index = lax.axis_index("shard")
    pair_side = shard_index % 2
    head_index = shard_index // 2
    block_index = shard_index % (2 * group_size) // 2
    local_rows, local_width = trunk_out.shape
    features = lax.all_gather(trunk_out, "member", axis=1, tiled=True)
    gathered = lax.all_gather(features, "shard", axis=0, tiled=True)
    tok_count, model_width = gathered.shape
    half_width = model_width // 2
    half_rows = tok_count // 2
    half_head = HD // 2
    row_block = half_width // group_size
    scale_factor = 1.0 / math.sqrt(HD)
    group_bits = list(range((2 * group_size).bit_length() - 1))
    query_piece = w_query[0, 0]
    kv_piece = w_key_value[0, 0]
    out_rows = w_out[0]
    gain_vector = norm_gain[0]
    head_weight = reward_weight[0]
    positions = jnp.arange(tok_count)
    own_start = pair_side * half_rows
    own_positions = own_start + jnp.arange(half_rows)
    own_segments = lax.dynamic_slice_in_dim(segment_ids, own_start, half_rows, 0)
    allowed = (own_segments[:, None] == segment_ids[None, :]) & (
        positions[None, :] <= own_positions[:, None]
    )
    member_of = jnp.arange(SEQS)[:, None] == segment_ids[None, :]
    pooling = member_of.astype(jnp.bfloat16)
    lengths = jnp.sum(member_of.astype(jnp.float32), axis=1)
    own_pooling = lax.dynamic_slice_in_dim(pooling, own_start, half_rows, 1)
    half_features = lax.dynamic_slice_in_dim(gathered, pair_side * half_width, half_width, 1)
    query_partial = jnp.dot(half_features, query_piece, preferred_element_type=jnp.float32)
    kept_rows = lax.dynamic_slice_in_dim(query_partial, own_start, half_rows, 0)
    sent_rows = lax.dynamic_slice_in_dim(query_partial, half_rows - own_start, half_rows, 0)
    queries = (kept_rows + partner_swap(sent_rows, 0)).astype(jnp.bfloat16)
    kv_features = lax.dynamic_slice_in_dim(half_features, block_index * row_block, row_block, 1)
    kv_values = group_total(
        jnp.dot(kv_features, kv_piece, preferred_element_type=jnp.float32), group_bits
    ).astype(jnp.bfloat16)
    key_full = kv_values[:, :HD]
    value_full = kv_values[:, HD:]
    raw_scores = (
        jnp.einsum("td,sd->ts", queries, key_full, preferred_element_type=jnp.float32)
        * scale_factor
    )
    capped = softcap_limit * jnp.tanh(raw_scores / softcap_limit)
    weights_exp = jnp.where(allowed, jnp.exp(capped), 0.0)
    attention = weights_exp / jnp.sum(weights_exp, axis=1, keepdims=True)
    attention_low = attention.astype(jnp.bfloat16)
    attended = jnp.dot(attention_low, value_full, preferred_element_type=jnp.float32).astype(
        jnp.bfloat16
    )
    seq_part = jnp.dot(own_pooling, attended, preferred_element_type=jnp.float32)
    seq_total = seq_part + partner_swap(seq_part, 0)
    seq_mean = (seq_total / lengths[:, None]).astype(jnp.bfloat16)
    own_dims = lax.dynamic_slice_in_dim(seq_mean, pair_side * half_head, half_head, 1)
    head_part = jnp.dot(own_dims, out_rows, preferred_element_type=jnp.float32)
    pooled_attn = lax.psum(head_part, "shard")
    pooled_input = jnp.dot(pooling, gathered, preferred_element_type=jnp.float32) / lengths[:, None]
    hidden = pooled_input + pooled_attn
    inverse_rms = lax.rsqrt(jnp.mean(hidden * hidden, axis=1) + norm_eps)
    normed = hidden * inverse_rms[:, None] * gain_vector
    rewards = jnp.sum(normed * head_weight, axis=1)
    seq_ids = jnp.arange(SEQS)
    chosen = (pair_order[0::2][:, None] == seq_ids[None, :]).astype(jnp.float32)
    rejected = (pair_order[1::2][:, None] == seq_ids[None, :]).astype(jnp.float32)
    margin = jnp.sum(chosen * rewards, axis=1) - jnp.sum(rejected * rewards, axis=1)
    pair_slope = loss_scale * jax.nn.sigmoid(-margin)
    reward_grad = jnp.sum(rejected * pair_slope[:, None], axis=0) - jnp.sum(
        chosen * pair_slope[:, None], axis=0
    )
    scaled_grad = reward_grad[:, None] * head_weight * gain_vector
    hidden_grad = inverse_rms[:, None] * (
        scaled_grad
        - hidden * (inverse_rms**2)[:, None] * jnp.mean(hidden * scaled_grad, axis=1, keepdims=True)
    )
    per_token = hidden_grad / lengths[:, None]
    grad_low = hidden_grad.astype(jnp.bfloat16)
    grad_dims = (
        jnp.einsum("jd,ed->je", grad_low, out_rows, preferred_element_type=jnp.float32)
        / lengths[:, None]
    )
    mean_grad = pair_join(grad_dims, partner_swap(grad_dims, 0), pair_side, 1)
    out_grad = jnp.take(mean_grad, own_segments, axis=0).astype(jnp.bfloat16)
    prob_grad = jnp.einsum("td,sd->ts", out_grad, value_full, preferred_element_type=jnp.float32)
    score_grad = attention * (prob_grad - jnp.sum(attention * prob_grad, axis=1, keepdims=True))
    raw_grad = (score_grad * (1.0 - (capped / softcap_limit) ** 2) * scale_factor).astype(
        jnp.bfloat16
    )
    query_grad = jnp.dot(raw_grad, key_full, preferred_element_type=jnp.float32).astype(
        jnp.bfloat16
    )
    key_grad = jnp.einsum("ts,td->sd", raw_grad, queries, preferred_element_type=jnp.float32)
    value_grad = jnp.einsum(
        "ts,td->sd", attention_low, out_grad, preferred_element_type=jnp.float32
    )
    kv_grad = group_total(jnp.concatenate([key_grad, value_grad], axis=1), group_bits).astype(
        jnp.bfloat16
    )
    query_wire = lax.optimization_barrier(query_grad).astype(jnp.float32)
    query_all = pair_join(
        query_grad, partner_swap(query_wire, 0).astype(jnp.bfloat16), pair_side, 0
    )
    grad_half = jnp.einsum("td,rd->tr", query_all, query_piece, preferred_element_type=jnp.float32)
    kv_term = jnp.einsum("te,re->tr", kv_grad, kv_piece, preferred_element_type=jnp.float32)
    start_col = block_index * row_block
    grad_half = lax.dynamic_update_slice_in_dim(
        grad_half,
        lax.dynamic_slice_in_dim(grad_half, start_col, row_block, 1) + kv_term,
        start_col,
        1,
    )
    pair_rows = 2 * local_rows
    start_row = head_index * pair_rows
    pair_segments = lax.dynamic_slice_in_dim(segment_ids, start_row, pair_rows, 0)
    token_half = lax.dynamic_slice_in_dim(per_token, pair_side * half_width, half_width, 1)
    direct = jnp.take(token_half, pair_segments, axis=0)
    grad_half = lax.dynamic_update_slice_in_dim(
        grad_half,
        lax.dynamic_slice_in_dim(grad_half, start_row, pair_rows, 0) + direct,
        start_row,
        0,
    )
    by_member = lax.psum_scatter(grad_half, "member", scatter_dimension=0, tiled=True)
    member_rows = by_member.shape[0]
    placed = lax.dynamic_update_slice_in_dim(
        jnp.zeros((member_rows, model_width), jnp.float32), by_member, pair_side * half_width, 1
    )
    trunk_grad = lax.psum_scatter(placed, "shard", scatter_dimension=1, tiled=True)
    return (trunk_grad, rewards[None])


def solution(mesh):
    placed = (
        P("shard", "member"),
        P(),
        P(),
        P("member", "shard", None, None),
        P("member", "shard", None, None),
        P("member", "shard", None),
        P("member", None),
        P("member", None),
    )
    return jax.shard_map(
        on_device,
        mesh=mesh,
        in_specs=placed,
        out_specs=(P("member", "shard"), P("member", None)),
        check_vma=False,
    )
```

profile of v0, /device:TPU:0, one launch (start us, length us, event | category | flops | bytes accessed | tf_op | source)
XLA Modules:
  0.0 226.3 jit_solution(8891735521188320311)
XLA Ops:
  7.2 12.1 %all_gather.6 = bf16[16,8192]{1,0:T(8,128)(2,1)} all-gather(bf16[16,2048]{1,0:T(8,128)(2,1)} %param.8), channel_id=1, replica_groups=mesh['member'=4,'shard'=8] {'member'}, dimensions={1}, use_global_device_ids=true | all-gather | bytes 327680 | tf_op jit(solution)/shard_map/all_gather | solution.py:52
  19.5 0.7 compare_and_fusion.1
  20.3 0.7 iota_compare_fusion.1
  20.9 28.0 %all-gather.2.cloned.1.call-done = bf16[128,8192]{1,0:T(8,128)(2,1)} async-done(((bf16[16,8192]{1,0:T(8,128)(2,1)}), bf16[128,8192]{1,0:T(8,128)(2,1)}) %all-gather.2.cloned.1.call-update) | async-done | bytes 2097168 | tf_op jit(solution)/shard_map/all_gather | solution.py:53
  49.0 1.4 fusion.13
  50.7 1.6 fusion.9
  52.4 1.5 collective-permute-start.2
  53.9 4.2 %collective-permute-done.2 = f32[128,256]{1,0:T(8,128)S(1)} collective-permute-done((f32[128,256]{1,0:T(8,128)S(1)}, f32[128,256]{1,0:T(8,128)S(1)}, u32[]{:S(2)}, u32[]{:S(2)}) %collective-permute-start.2) | collective-permute-done | bytes 131104 | tf_op jit(solution)/shard_map/ppermute | solution.py:21
  58.2 1.9 collective-permute-start.3
  60.0 6.7 %collective-permute-done.3 = f32[128,256]{1,0:T(8,128)S(1)} collective-permute-done((f32[128,256]{1,0:T(8,128)S(1)}, f32[128,256]{1,0:T(8,128)S(1)}, u32[]{:S(2)}, u32[]{:S(2)}) %collective-permute-start.3) | collective-permute-done | bytes 131104 | tf_op jit(solution)/shard_map/ppermute | solution.py:21
  67.1 0.3 fusion.3
  67.5 1.0 collective-permute-done.4
  68.7 2.2 fusion.5
  71.3 54.7 %all-reduce.2.cloned.1.call-done = f32[8,8192]{1,0:T(8,128)} async-done(((f32[8,8192]{1,0:T(8,128)}), f32[8,8192]{1,0:T(8,128)}) %all-reduce.2.cloned.1.call-update) | async-done | bytes 262160 | tf_op jit(solution)/shard_map/psum | solution.py:104
  126.0 1.5 multiply_reduce_fusion.2
  128.5 0.4 convolution_divide_fusion.1
  129.0 1.5 gather_fusion.1
  130.6 0.6 gather_fusion
  131.5 0.3 multiply_reduce_fusion.3
  132.2 0.6 collective-permute-start.7
  132.9 0.8 collective-permute-done.7
  133.7 0.6 collective-permute-start.8
  134.4 5.2 %collective-permute-done.8 = f32[128,256]{0,1:T(8,128)S(1)} collective-permute-done((f32[128,256]{0,1:T(8,128)S(1)}, f32[128,256]{0,1:T(8,128)S(1)}, u32[]{:S(2)}, u32[]{:S(2)}) %collective-permute-start.8) | collective-permute-done | bytes 131104 | tf_op jit(solution)/shard_map/ppermute | solution.py:21
  139.6 1.5 collective-permute-start.9
  141.1 0.4 fusion.7
  141.6 6.7 %collective-permute-done.9 = f32[128,256]{0,1:T(8,128)S(1)} collective-permute-done((f32[128,256]{0,1:T(8,128)S(1)}, f32[128,256]{0,1:T(8,128)S(1)}, u32[]{:S(2)}, u32[]{:S(2)}) %collective-permute-start.9) | collective-permute-done | bytes 131104 | tf_op jit(solution)/shard_map/ppermute | solution.py:21
  148.3 0.3 fusion.1
  148.7 1.3 copy-done.1
  150.1 34.3 %reduce-scatter.3.cloned.1.call-done = f32[32,4096]{1,0:T(8,128)} async-done(((f32[128,4096]{1,0:T(8,128)}), f32[32,4096]{1,0:T(8,128)}) %reduce-scatter.3.cloned.1.call-update) | async-done | bytes 524304 | tf_op jit(solution)/shard_map/reduce_scatter | solution.py:170
  184.5 1.1 constant_dynamic-update-slice_fusion
  185.6 1.0 copy-done.4
  186.6 33.2 %reduce-scatter.5.cloned.1.call-done = f32[32,1024]{1,0:T(8,128)} async-done(((f32[32,8192]{1,0:T(8,128)}), f32[32,1024]{1,0:T(8,128)}) %reduce-scatter.5.cloned.1.call-update) | async-done | bytes 131088 | tf_op jit(solution)/shard_map/reduce_scatter | solution.py:175
  (76 shorter events, 3.5 us)
Async XLA Ops:
  7.2 43.5 %copy-start = (bf16[1,1,4096,128]{3,2,1,0:T(8,128)(2,1)S(1)}, bf16[1,1,4096,128]{3,2,1,0:T(8,128)(2,1)}, u32[]{:S(2)}) copy-start(bf16[1,1,4096,128]{3,2,1,0:T(8,128)(2,1)} %param.11) | copy-start | bytes 3145732
  7.2 41.8 %all-gather.2.cloned.1.call-start = ((), (), s32[]{:S(2)}) async-start(), calls=%async_computation.2 | async-start | bytes 2359296 | tf_op jit(solution)/shard_map/all_gather | solution.py:53
  19.4 106.6 %all-reduce.2.cloned.1.call-start = ((), (), s32[]{:S(2)}) async-start(), calls=%async_computation.3 | async-start | bytes 524288 | tf_op jit(solution)/shard_map/psum | solution.py:104
  20.9 45.9 %copy-start.9 = (s32[128]{0:T(128)S(1)}, s32[128]{0:T(128)}, u32[]{:S(2)}) copy-start(s32[128]{0:T(128)} %param.9) | copy-start | bytes 1540
  50.4 2.0 collective-permute-start.1
  52.3 18.7 %copy-start.11 = (s32[8]{0:T(128)S(1)}, s32[8]{0:T(128)}, u32[]{:S(2)}) copy-start(s32[8]{0:T(128)} %param.10) | copy-start | bytes 100
  52.3 73.6 %copy-start.2 = (bf16[128,8192]{1,0:T(8,128)(2,1)S(1)}, bf16[128,8192]{1,0:T(8,128)(2,1)}, u32[]{:S(2)}) copy-start(bf16[128,8192]{1,0:T(8,128)(2,1)} %all-gather.2.cloned.1.call-done) | copy-start | bytes 6291460
  52.4 5.8 %collective-permute-start.2 = (f32[128,256]{1,0:T(8,128)S(1)}, f32[128,256]{1,0:T(8,128)S(1)}, u32[]{:S(2)}, u32[]{:S(2)}) collective-permute-start(f32[128,256]{1,0:T(8,128)S(1)} %add.127), channel_id=1, source_target_pairs={{0,2},{2,0},{1,3},{3,1},{4,6},{6,4},{5,7},{7,5},{8,10},{10,8},{9,1... | collective-permute-start | bytes 393224 | tf_op jit(solution)/shard_map/ppermute | solution.py:21
  53.9 6.1 %collective-permute-start = (f32[64,128]{1,0:T(8,128)S(1)}, f32[64,128]{1,0:T(8,128)S(1)}, u32[]{:S(2)}, u32[]{:S(2)}) collective-permute-start(f32[64,128]{1,0:T(8,128)S(1)} %constant_dynamic-slice_fusion.1), channel_id=1, source_target_pairs={{0,1},{1,0},{2,3},{3,2},{4,5},{5,4},{6,7},{7,6},{8,9},{9,8},{10,11... | collective-permute-start | bytes 98312 | tf_op jit(solution)/shard_map/ppermute | solution.py:21
  58.2 8.6 %collective-permute-start.3 = (f32[128,256]{1,0:T(8,128)S(1)}, f32[128,256]{1,0:T(8,128)S(1)}, u32[]{:S(2)}, u32[]{:S(2)}) collective-permute-start(f32[128,256]{1,0:T(8,128)S(1)} %add.128), channel_id=1, source_target_pairs={{0,4},{4,0},{1,5},{5,1},{2,6},{6,2},{3,7},{7,3},{8,12},{12,8},{9,1... | collective-permute-start | bytes 393224 | tf_op jit(solution)/shard_map/ppermute | solution.py:21
  67.4 1.2 collective-permute-start.4
  68.7 58.9 %copy-start.7 = (f32[1,8192]{1,0:T(1,128)S(1)}, f32[1,8192]{1,0:T(1,128)}, u32[]{:S(2)}) copy-start(f32[1,8192]{1,0:T(1,128)} %param.15) | copy-start | bytes 98308
  68.7 58.9 %copy-start.8 = (f32[1,8192]{1,0:T(1,128)S(1)}, f32[1,8192]{1,0:T(1,128)}, u32[]{:S(2)}) copy-start(f32[1,8192]{1,0:T(1,128)} %param.14) | copy-start | bytes 98308
  70.9 113.5 %reduce-scatter.3.cloned.1.call-start = ((), (), s32[]{:S(2)}) async-start(), calls=%async_computation.4 | async-start | bytes 2621440 | tf_op jit(solution)/shard_map/reduce_scatter | solution.py:170
  126.0 2.6 %copy-start.3 = (bf16[1,64,8192]{2,1,0:T(8,128)(2,1)S(1)}, bf16[1,64,8192]{2,1,0:T(8,128)(2,1)}, u32[]{:S(2)}) copy-start(bf16[1,64,8192]{2,1,0:T(8,128)(2,1)} %param.13) | copy-start | bytes 3145732
  127.8 2.7 %copy-start.10 = (f32[8]{0:T(128)}, f32[8]{0:T(128)S(1)}, u32[]{:S(2)}) copy-start(f32[8]{0:T(128)S(1)} %multiply_reduce_fusion.1) | copy-start | bytes 100
  128.9 1.6 collective-permute-start.5
  132.2 16.1 %copy-start.6 = (bf16[1,1,1024,256]{3,2,1,0:T(8,128)(2,1)S(1)}, bf16[1,1,1024,256]{3,2,1,0:T(8,128)(2,1)}, u32[]{:S(2)}) copy-start(bf16[1,1,1024,256]{3,2,1,0:T(8,128)(2,1)} %param.12) | copy-start | bytes 1572868
  132.2 1.5 collective-permute-start.7
  132.9 1.5 collective-permute-start.6
  133.7 5.8 %collective-permute-start.8 = (f32[128,256]{0,1:T(8,128)S(1)}, f32[128,256]{0,1:T(8,128)S(1)}, u32[]{:S(2)}, u32[]{:S(2)}) collective-permute-start(f32[128,256]{0,1:T(8,128)S(1)} %fusion.40), channel_id=1, source_target_pairs={{0,2},{2,0},{1,3},{3,1},{4,6},{6,4},{5,7},{7,5},{8,10},{10,8},{9,1... | collective-permute-start | bytes 393224 | tf_op jit(solution)/shard_map/ppermute | solution.py:21
  139.6 8.7 %collective-permute-start.9 = (f32[128,256]{0,1:T(8,128)S(1)}, f32[128,256]{0,1:T(8,128)S(1)}, u32[]{:S(2)}, u32[]{:S(2)}) collective-permute-start(f32[128,256]{0,1:T(8,128)S(1)} %add.137), channel_id=1, source_target_pairs={{0,4},{4,0},{1,5},{5,1},{2,6},{6,2},{3,7},{7,3},{8,12},{12,8},{9,1... | collective-permute-start | bytes 393224 | tf_op jit(solution)/shard_map/ppermute | solution.py:21
  141.1 7.5 %copy-start.5 = (f32[32,4096]{1,0:T(8,128)S(1)}, f32[32,4096]{1,0:T(8,128)}, u32[]{:S(2)}) copy-start(f32[32,4096]{1,0:T(8,128)} %gather_fusion.1) | copy-start | bytes 1572868
  148.7 1.3 copy-start.1
  150.1 69.7 %reduce-scatter.5.cloned.1.call-start = ((), (), s32[]{:S(2)}) async-start(), calls=%async_computation.5 | async-start | bytes 1179648 | tf_op jit(solution)/shard_map/reduce_scatter | solution.py:175
  185.6 1.0 copy-start.4
Sparse Core Ops, SparseCore 0:
  19.5 29.4 all-gather.1
  71.0 54.8 all-reduce.1
  150.2 34.1 reduce-scatter.2
  187.1 32.6 reduce-scatter.4
where the time goes:
time: 227 us; the launch traced here: 226 us
  waiting for transfers between devices  175 us (77%)
  between operations  14.1 us (6%)
  blocking collectives  12.1 us (5%)
  matrix products  9.47 us (4%)
  starting transfers between devices  6.59 us (3%)
  local copies, waits for them, and re-layouts  5.82 us (3%)
  other arithmetic  3.18 us (1%)
    psum x1, waiting for transfers between devices, on_device(): pooled_attn = lax.psum(head_part, 'shard')  54.7 us
    reduce_scatter x1, waiting for transfers between devices, on_device(): lax.psum_scatter(grad_half, 'member', scatter_dimension=0, tiled=True)  34.3 us
    reduce_scatter x1, waiting for transfers between devices, on_device(): lax.psum_scatter(placed, 'shard', scatter_dimension=1, tiled=True)  33.2 us
    all_gather x1, waiting for transfers between devices, on_device(): gathered = lax.all_gather(features, 'shard', axis=0, tiled=True)  28 us
    ppermute x10, waiting for transfers between devices, from_partner(): return lax.ppermute(block, axis, route)  24.7 us
    all_gather x1, blocking collectives, on_device(): features = lax.all_gather(trunk_out, 'member', axis=1, tiled=True)  12.1 us
    ppermute x10, starting transfers between devices, from_partner(): return lax.ppermute(block, axis, route)  6.43 us
  transfers between devices with their start and end apart: 14, of which 10 were waited for; matrix products, arithmetic and copies ran while one was open for 2% of the time, Pallas kernels for 0%

commit v1 on v0

--- a/solution.py
+++ b/solution.py
@@ -50,7 +50,18 @@
     block_index = shard_index % (2 * group_size) // 2
     local_rows, local_width = trunk_out.shape
     features = lax.all_gather(trunk_out, "member", axis=1, tiled=True)
-    gathered = lax.all_gather(features, "shard", axis=0, tiled=True)
+    opened = lax.axis_size("shard")
+    x_new = lax.axis_index("shard")
+    part_now, val2, y = (opened, x_new, features.shape[0])
+    y1, everything = (features, 1)
+    while everything < part_now:
+        column = []
+        for u in tuple(range(part_now)):
+            column.append((u, (u - everything) % part_now))
+        wide_out = lax.ppermute(y1, axis_name="shard", perm=column)
+        y1 = jnp.concatenate([y1, wide_out], 0)
+        everything = 2 * everything
+    gathered = jnp.roll(y1, val2 * y, 0)
     tok_count, model_width = gathered.shape
     half_width = model_width // 2
     half_rows = tok_count // 2

time: 227 us -> 269 us (1.19)
  waiting for transfers between devices: 175 us -> 209 us
  local copies, waits for them, and re-layouts: 5.82 us -> 12.5 us
    ppermute x0 -> x3, waiting for transfers between devices: none -> 60.3 us  [on_device(): wide_out = lax.ppermute(y1, axis_name='shard', perm=column)]
    all_gather x1 -> x0, waiting for transfers between devices: 28 us -> none  [on_device(): gathered = lax.all_gather(features, 'shard', axis=0, tiled=True)]
    unnamed x24 -> x29, local copies, waits for them, and re-layouts: 2.35 us -> 7.94 us
    ppermute x0 -> x3, starting transfers between devices: none -> 4.55 us  [on_device(): wide_out = lax.ppermute(y1, axis_name='shard', perm=column)]
  transfers between devices with their start and end apart: 14 -> 16, of which waited for: 10 -> 12; matrix products, arithmetic and copies ran while one was open for 2% -> 3% of each run, Pallas kernels for 0% -> 0%
where the time goes in v1:
time: 269 us
  waiting for transfers between devices  209 us (78%)
  between operations  14 us (5%)
  local copies, waits for them, and re-layouts  12.5 us (5%)
  blocking collectives  10.9 us (4%)
  matrix products  9.97 us (4%)
  starting transfers between devices  9.1 us (3%)
  other arithmetic  3.27 us (1%)
    ppermute x3, waiting for transfers between devices, on_device(): wide_out = lax.ppermute(y1, axis_name='shard', perm=column)  60.3 us
    psum x1, waiting for transfers between devices, on_device(): pooled_attn = lax.psum(head_part, 'shard')  54 us
    reduce_scatter x1, waiting for transfers between devices, on_device(): lax.psum_scatter(grad_half, 'member', scatter_dimension=0, tiled=True)  34.3 us
    reduce_scatter x1, waiting for transfers between devices, on_device(): lax.psum_scatter(placed, 'shard', scatter_dimension=1, tiled=True)  33.4 us
    ppermute x10, waiting for transfers between devices, from_partner(): return lax.ppermute(block, axis, route)  26.9 us
    all_gather x1, blocking collectives, on_device(): features = lax.all_gather(trunk_out, 'member', axis=1, tiled=True)  10.9 us
    unnamed x29, local copies, waits for them, and re-layouts  7.94 us
  transfers between devices with their start and end apart: 16, of which 12 were waited for; matrix products, arithmetic and copies ran while one was open for 3% of the time, Pallas kernels for 0%

profile of v1, /device:TPU:0, one launch (start us, length us, event | category | flops | bytes accessed | tf_op | source)
XLA Modules:
  0.0 268.6 jit_solution(5610089000873011667)
XLA Ops:
  7.2 10.9 %all_gather.3 = bf16[16,8192]{1,0:T(8,128)(2,1)S(1)} all-gather(bf16[16,2048]{1,0:T(8,128)(2,1)} %param.8), channel_id=1, replica_groups=mesh['member'=4,'shard'=8] {'member'}, dimensions={1}, use_global_device_ids=true | all-gather | bytes 327680 | tf_op jit(solution)/shard_map/all_gather | solution.py:52
  18.1 1.3 collective-permute-start
  20.1 0.7 compare_and_fusion.1
  20.9 2.4 collective-permute-done
  23.3 2.4 collective-permute-start.1
  26.4 11.4 %collective-permute-done.1 = bf16[32,8192]{1,0:T(8,128)(2,1)S(1)} collective-permute-done((bf16[32,8192]{1,0:T(8,128)(2,1)S(1)}, bf16[32,8192]{1,0:T(8,128)(2,1)S(1)}, u32[]{:S(2)}, u32[]{:S(2)}) %collective-permute-start.1) | collective-permute-done | bytes 524320 | tf_op jit(solution)/shard_map/ppermute | solution.py:61
  37.9 0.9 collective-permute-start.2
  39.5 0.8 constant_dynamic-update-slice_fusion.5
  40.3 46.4 %collective-permute-done.2 = bf16[64,8192]{1,0:T(8,128)(2,1)S(1)} collective-permute-done((bf16[64,8192]{1,0:T(8,128)(2,1)S(1)}, bf16[64,8192]{1,0:T(8,128)(2,1)S(1)}, u32[]{:S(2)}, u32[]{:S(2)}) %collective-permute-start.2) | collective-permute-done | bytes 1048608 | tf_op jit(solution)/shard_map/ppermute | solution.py:61
  86.7 1.1 constant_dynamic-update-slice_fusion.4
  89.2 0.8 constant_dynamic-update-slice_fusion.1
  90.1 1.1 constant_dynamic-update-slice_fusion
  91.1 1.3 fusion.14
  92.5 1.9 fusion.10
  95.1 5.3 %collective-permute-done.5 = f32[128,256]{1,0:T(8,128)S(1)} collective-permute-done((f32[128,256]{1,0:T(8,128)S(1)}, f32[128,256]{1,0:T(8,128)S(1)}, u32[]{:S(2)}, u32[]{:S(2)}) %collective-permute-start.5) | collective-permute-done | bytes 131104 | tf_op jit(solution)/shard_map/ppermute | solution.py:21
  100.4 1.0 collective-permute-start.6
  101.4 7.8 %collective-permute-done.6 = f32[128,256]{1,0:T(8,128)S(1)} collective-permute-done((f32[128,256]{1,0:T(8,128)S(1)}, f32[128,256]{1,0:T(8,128)S(1)}, u32[]{:S(2)}, u32[]{:S(2)}) %collective-permute-start.6) | collective-permute-done | bytes 131104 | tf_op jit(solution)/shard_map/ppermute | solution.py:21
  110.0 1.0 collective-permute-done.7
  111.1 1.0 fusion.6
  112.5 54.0 %all-reduce.2.cloned.1.call-done = f32[8,8192]{1,0:T(8,128)} async-done(((f32[8,8192]{1,0:T(8,128)}), f32[8,8192]{1,0:T(8,128)}) %all-reduce.2.cloned.1.call-update) | async-done | bytes 262160 | tf_op jit(solution)/shard_map/psum | solution.py:115
  166.5 2.1 multiply_reduce_fusion.2
  170.1 1.5 gather_fusion.1
  174.0 0.8 collective-permute-done.10
  175.5 5.2 %collective-permute-done.11 = f32[128,256]{0,1:T(8,128)S(1)} collective-permute-done((f32[128,256]{0,1:T(8,128)S(1)}, f32[128,256]{0,1:T(8,128)S(1)}, u32[]{:S(2)}, u32[]{:S(2)}) %collective-permute-start.11) | collective-permute-done | bytes 131104 | tf_op jit(solution)/shard_map/ppermute | solution.py:21
  180.7 1.5 collective-permute-start.12
  182.6 6.7 %collective-permute-done.12 = f32[128,256]{0,1:T(8,128)S(1)} collective-permute-done((f32[128,256]{0,1:T(8,128)S(1)}, f32[128,256]{0,1:T(8,128)S(1)}, u32[]{:S(2)}, u32[]{:S(2)}) %collective-permute-start.12) | collective-permute-done | bytes 131104 | tf_op jit(solution)/shard_map/ppermute | solution.py:21
  189.3 1.4 fusion.2
  190.8 1.3 copy-done.1
  192.2 34.3 %reduce-scatter.3.cloned.1.call-done = f32[32,4096]{1,0:T(8,128)} async-done(((f32[128,4096]{1,0:T(8,128)}), f32[32,4096]{1,0:T(8,128)}) %reduce-scatter.3.cloned.1.call-update) | async-done | bytes 524304 | tf_op jit(solution)/shard_map/reduce_scatter | solution.py:181
  226.6 1.1 constant_dynamic-update-slice_fusion.8
  227.7 1.0 copy-done.3
  228.7 33.4 %reduce-scatter.5.cloned.1.call-done = f32[32,1024]{1,0:T(8,128)} async-done(((f32[32,8192]{1,0:T(8,128)}), f32[32,1024]{1,0:T(8,128)}) %reduce-scatter.5.cloned.1.call-update) | async-done | bytes 131088 | tf_op jit(solution)/shard_map/reduce_scatter | solution.py:186
  (87 shorter events, 10.8 us)
Async XLA Ops:
  7.2 85.3 %copy-start = (bf16[1,1,4096,128]{3,2,1,0:T(8,128)(2,1)S(1)}, bf16[1,1,4096,128]{3,2,1,0:T(8,128)(2,1)}, u32[]{:S(2)}) copy-start(bf16[1,1,4096,128]{3,2,1,0:T(8,128)(2,1)} %param.11) | copy-start | bytes 3145732
  7.2 159.3 %all-reduce.2.cloned.1.call-start = ((), (), s32[]{:S(2)}) async-start(), calls=%async_computation.2 | async-start | bytes 524288 | tf_op jit(solution)/shard_map/psum | solution.py:115
  18.1 5.2 %collective-permute-start = (bf16[16,8192]{1,0:T(8,128)(2,1)S(1)}, bf16[16,8192]{1,0:T(8,128)(2,1)S(1)}, u32[]{:S(2)}, u32[]{:S(2)}) collective-permute-start(bf16[16,8192]{1,0:T(8,128)(2,1)S(1)} %all_gather.3), channel_id=1, source_target_pairs={{0,7},{1,0},{2,1},{3,2},{4,3},{5,4},{6,5},{7,6},{8,15},{9,8},{10,9... | collective-permute-start | bytes 786440 | tf_op jit(solution)/shard_map/ppermute | solution.py:61
  23.3 14.4 %collective-permute-start.1 = (bf16[32,8192]{1,0:T(8,128)(2,1)S(1)}, bf16[32,8192]{1,0:T(8,128)(2,1)S(1)}, u32[]{:S(2)}, u32[]{:S(2)}) collective-permute-start(bf16[32,8192]{1,0:T(8,128)(2,1)S(1)} %pad_maximum_fusion.1), channel_id=1, source_target_pairs={{0,6},{1,7},{2,0},{3,1},{4,2},{5,3},{6,4},{7,5},{8,14},{9,15},{10,... | collective-permute-start | bytes 1572872 | tf_op jit(solution)/shard_map/ppermute | solution.py:61
  37.9 53.3 %copy-start.5 = (bf16[1,1,1024,256]{3,2,1,0:T(8,128)(2,1)S(1)}, bf16[1,1,1024,256]{3,2,1,0:T(8,128)(2,1)}, u32[]{:S(2)}) copy-start(bf16[1,1,1024,256]{3,2,1,0:T(8,128)(2,1)} %param.12) | copy-start | bytes 1572868
  37.9 48.9 %collective-permute-start.2 = (bf16[64,8192]{1,0:T(8,128)(2,1)S(1)}, bf16[64,8192]{1,0:T(8,128)(2,1)S(1)}, u32[]{:S(2)}, u32[]{:S(2)}) collective-permute-start(bf16[64,8192]{1,0:T(8,128)(2,1)S(1)} %pad_maximum_fusion), channel_id=1, source_target_pairs={{0,4},{1,5},{2,6},{3,7},{4,0},{5,1},{6,2},{7,3},{8,12},{9,13},{10,... | collective-permute-start | bytes 3145736 | tf_op jit(solution)/shard_map/ppermute | solution.py:61
  87.8 21.5 %copy-start.8 = (s32[128]{0:T(128)S(1)}, s32[128]{0:T(128)}, u32[]{:S(2)}) copy-start(s32[128]{0:T(128)} %param.9) | copy-start | bytes 1540
  88.5 22.6 %copy-start.2 = (bf16[1,64,8192]{2,1,0:T(8,128)(2,1)S(1)}, bf16[1,64,8192]{2,1,0:T(8,128)(2,1)}, u32[]{:S(2)}) copy-start(bf16[1,64,8192]{2,1,0:T(8,128)(2,1)} %param.13) | copy-start | bytes 3145732
  90.1 22.2 %copy-start.10 = (s32[8]{0:T(128)S(1)}, s32[8]{0:T(128)}, u32[]{:S(2)}) copy-start(s32[8]{0:T(128)} %param.10) | copy-start | bytes 100
  92.4 76.2 %copy-start.6 = (f32[1,8192]{1,0:T(1,128)S(1)}, f32[1,8192]{1,0:T(1,128)}, u32[]{:S(2)}) copy-start(f32[1,8192]{1,0:T(1,128)} %param.15) | copy-start | bytes 98308
  92.4 76.2 %copy-start.7 = (f32[1,8192]{1,0:T(1,128)S(1)}, f32[1,8192]{1,0:T(1,128)}, u32[]{:S(2)}) copy-start(f32[1,8192]{1,0:T(1,128)} %param.14) | copy-start | bytes 98308
  92.4 2.0 collective-permute-start.4
  94.5 6.0 %collective-permute-start.5 = (f32[128,256]{1,0:T(8,128)S(1)}, f32[128,256]{1,0:T(8,128)S(1)}, u32[]{:S(2)}, u32[]{:S(2)}) collective-permute-start(f32[128,256]{1,0:T(8,128)S(1)} %add.141), channel_id=1, source_target_pairs={{0,2},{2,0},{1,3},{3,1},{4,6},{6,4},{5,7},{7,5},{8,10},{10,8},{9,1... | collective-permute-start | bytes 393224 | tf_op jit(solution)/shard_map/ppermute | solution.py:21
  94.6 6.8 %collective-permute-start.3 = (f32[64,128]{1,0:T(8,128)S(1)}, f32[64,128]{1,0:T(8,128)S(1)}, u32[]{:S(2)}, u32[]{:S(2)}) collective-permute-start(f32[64,128]{1,0:T(8,128)S(1)} %constant_dynamic-slice_fusion.1), channel_id=1, source_target_pairs={{0,1},{1,0},{2,3},{3,2},{4,5},{5,4},{6,7},{7,6},{8,9},{9,8},{10,11... | collective-permute-start | bytes 98312 | tf_op jit(solution)/shard_map/ppermute | solution.py:21
  100.4 8.8 %collective-permute-start.6 = (f32[128,256]{1,0:T(8,128)S(1)}, f32[128,256]{1,0:T(8,128)S(1)}, u32[]{:S(2)}, u32[]{:S(2)}) collective-permute-start(f32[128,256]{1,0:T(8,128)S(1)} %add.142), channel_id=1, source_target_pairs={{0,4},{4,0},{1,5},{5,1},{2,6},{6,2},{3,7},{7,3},{8,12},{12,8},{9,1... | collective-permute-start | bytes 393224 | tf_op jit(solution)/shard_map/ppermute | solution.py:21
  109.9 1.2 collective-permute-start.7
  112.2 114.3 %reduce-scatter.3.cloned.1.call-start = ((), (), s32[]{:S(2)}) async-start(), calls=%async_computation.3 | async-start | bytes 2621440 | tf_op jit(solution)/shard_map/reduce_scatter | solution.py:181
  168.9 4.4 %copy-start.9 = (f32[8]{0:T(128)}, f32[8]{0:T(128)S(1)}, u32[]{:S(2)}) copy-start(f32[8]{0:T(128)S(1)} %multiply_reduce_fusion.1) | copy-start | bytes 100
  170.0 1.6 collective-permute-start.8
  172.3 18.4 %copy-start.4 = (f32[32,4096]{1,0:T(8,128)S(1)}, f32[32,4096]{1,0:T(8,128)}, u32[]{:S(2)}) copy-start(f32[32,4096]{1,0:T(8,128)} %gather_fusion.1) | copy-start | bytes 1572868
  173.3 1.6 collective-permute-start.10
  173.9 1.5 collective-permute-start.9
  174.8 5.8 %collective-permute-start.11 = (f32[128,256]{0,1:T(8,128)S(1)}, f32[128,256]{0,1:T(8,128)S(1)}, u32[]{:S(2)}, u32[]{:S(2)}) collective-permute-start(f32[128,256]{0,1:T(8,128)S(1)} %fusion.40), channel_id=1, source_target_pairs={{0,2},{2,0},{1,3},{3,1},{4,6},{6,4},{5,7},{7,5},{8,10},{10,8},{9,1... | collective-permute-start | bytes 393224 | tf_op jit(solution)/shard_map/ppermute | solution.py:21
  180.7 8.7 %collective-permute-start.12 = (f32[128,256]{0,1:T(8,128)S(1)}, f32[128,256]{0,1:T(8,128)S(1)}, u32[]{:S(2)}, u32[]{:S(2)}) collective-permute-start(f32[128,256]{0,1:T(8,128)S(1)} %add.151), channel_id=1, source_target_pairs={{0,4},{4,0},{1,5},{5,1},{2,6},{6,2},{3,7},{7,3},{8,12},{12,8},{9,1... | collective-permute-start | bytes 393224 | tf_op jit(solution)/shard_map/ppermute | solution.py:21
  190.8 1.3 copy-start.1
  192.2 69.8 %reduce-scatter.5.cloned.1.call-start = ((), (), s32[]{:S(2)}) async-start(), calls=%async_computation.4 | async-start | bytes 1179648 | tf_op jit(solution)/shard_map/reduce_scatter | solution.py:186
  227.7 1.0 copy-start.3
Sparse Core Ops, SparseCore 0:
  112.3 54.1 all-reduce.1
  192.3 34.1 reduce-scatter.2
  229.4 32.6 reduce-scatter.4
